TPU v7x, 32 devices: a whole 2x2x4 slice. The times are simulated.
32 devices in a mesh: seq: 16 (over z, y, core), dp: 2 (over x).
Axes of the slice: x: 2, y: 2, z: 4, core: 2. Of those that a mesh axis runs over, the one named last changes fastest.
Arguments:
- queries: bfloat16 [2, 2048, 1024], P('dp', 'seq'), may hold values from -6 to 6
- keys: bfloat16 [2, 2048, 1024], P('dp', 'seq'), may hold values from -6 to 6
- values: bfloat16 [2, 2048, 1024], P('dp', 'seq'), may hold values from -6 to 6
- d_out: bfloat16 [2, 2048, 1024], P('dp', 'seq'), may hold values from -6 to 6
- segment_ids: int32 [2, 2048], P('dp', 'seq'), may hold values from 0 to 2, never falling along the last dimension, each value on 1 to 1536 neighbouring positions
- block_bucket: int32 [2, 16], P('dp', 'seq'), may hold values from 0 to 63
- block_mask: int32 [2, 16, 5, 1], P('dp', 'seq'), may hold values 0 or 1
- bias_table: bfloat16 [16, 64, 64], replicated, may hold values from -4 to 4
Outputs:
- attention_out: bfloat16 [2, 2048, 1024], P('dp', 'seq')
- d_queries: bfloat16 [2, 2048, 1024], P('dp', 'seq')
- d_keys: bfloat16 [2, 2048, 1024], P('dp', 'seq')
- d_values: bfloat16 [2, 2048, 1024], P('dp', 'seq')
- d_table: float32 [16, 64, 64], replicated
Inputs may be any that keep to these rules, and one draw needn't show every extreme that they name: `segment_ids`: each document is a run of consecutive tokens of one sequence.
All inputs are finite; a program needn't handle non-finite values. No bound on the sum of `block_mask` on one device may be relied on, other than what follows from the above.
Results may differ from a plain program's by a relative error of at most 0.024.
Values may be sent and summed in bfloat16 or wider, within the bound.
No kernel may reach another device: no remote copies, remote signals or barrier semaphores. Data moves between devices by JAX's collectives and lax.ppermute only.
A program may use at most 64 MiB of HBM per device.

v0:
```python
import jax
import jax.numpy as jnp
from jax import lax
from jax.sharding import PartitionSpec as P

H = 16
DH = 64
NB = 64
BLK = 128
masked_value = -1e30


def from_partner(value, axis, apart):
    mask = 2**apart
    pairs = [(source, source ^ mask) for source in range(lax.axis_size(axis))]
    return lax.ppermute(value, axis, pairs)


def expand_blocks(bias_block, row_count, col_count):
    leading = bias_block.shape[:-2]
    row_blocks = bias_block.shape[-2]
    col_blocks = bias_block.shape[-1]
    widened = jnp.broadcast_to(
        bias_block[..., :, None, :, None],
        leading + (row_blocks, row_count // row_blocks, col_blocks, col_count // col_blocks),
    )
    return widened.reshape(leading + (row_count, col_count))


def one_hot_rows(buckets):
    levels_all = jnp.arange(NB, dtype=jnp.float32)
    return (buckets.astype(jnp.float32)[:, None] == levels_all[None, :]).astype(jnp.bfloat16)


def bias_tile(bias_table, row_hot, col_hot):
    picked = jnp.einsum(
        "bn,hnm->hbm", row_hot, bias_table, preferred_element_type=jnp.float32
    ).astype(jnp.bfloat16)
    return jnp.einsum("hbm,cm->hbc", picked, col_hot, preferred_element_type=jnp.float32)


def allowed_pairs(seg_rows, seg_cols, block_ok):
    same_doc = seg_rows.astype(jnp.float32)[:, None] == seg_cols.astype(jnp.float32)[None, :]
    return same_doc & expand_blocks(block_ok, seg_rows.shape[0], seg_cols.shape[0])


def masked_scores(query_heads, key_heads, bias_block, allowed):
    products = jnp.einsum(
        "thd,uhd->htu", query_heads, key_heads, preferred_element_type=jnp.float32
    )
    shifted = products * 0.125 + expand_blocks(bias_block, query_heads.shape[0], key_heads.shape[0])
    return jnp.where(allowed[None], shifted, masked_value)


def grad_terms(scores, allowed, lse, row_delta, grad_heads, value_heads):
    probs = jnp.where(allowed[None], jnp.exp(scores - lse[:, :, None]), 0.0)
    dprob = jnp.einsum("thd,uhd->htu", grad_heads, value_heads, preferred_element_type=jnp.float32)
    dscore = probs * (dprob - row_delta[:, :, None])
    return (probs.astype(jnp.bfloat16), dscore)


def local(queries, keys, values, d_out, segment_ids, block_bucket, block_mask, bias_table):
    row_count = queries.shape[1]
    block_count = row_count // BLK
    level_count = lax.axis_size("seq").bit_length() - 1
    query_heads = queries[0].reshape(row_count, H, DH)
    grad_heads = d_out[0].reshape(row_count, H, DH)
    own_keys = keys[0]
    own_values = values[0]
    own_seg = segment_ids[0]
    own_bucket = block_bucket[0]
    own_mask = block_mask[0] != 0
    own_hot = one_hot_rows(own_bucket)
    own_hot_wide = own_hot.astype(jnp.float32)
    section_list = list(range(level_count + 1))
    stored = {}
    run_max = jnp.full((H, row_count), masked_value, jnp.float32)
    run_sum = jnp.zeros((H, row_count), jnp.float32)
    run_acc = jnp.zeros((row_count, H, DH), jnp.float32)
    for section_num in section_list:
        if section_num == 0:
            key_rows, value_rows, seg_cols, bucket_cols = (
                own_keys,
                own_values,
                own_seg,
                own_bucket,
            )
            block_ok = own_mask[:, 0, :] | jnp.eye(block_count, dtype=bool)
        else:
            key_rows, value_rows, seg_cols, bucket_cols = from_partner(
                (
                    own_keys,
                    own_values,
                    own_seg.astype(jnp.bfloat16),
                    own_bucket.astype(jnp.bfloat16),
                ),
                "seq",
                section_num - 1,
            )
            block_ok = own_mask[:, section_num, :]
        key_heads = key_rows.reshape(row_count, H, DH)
        value_heads = value_rows.reshape(row_count, H, DH)
        col_hot = one_hot_rows(bucket_cols)
        bias_block = bias_tile(bias_table, own_hot, col_hot)
        allowed = allowed_pairs(own_seg, seg_cols, block_ok)
        stored[section_num] = (key_heads, value_heads, seg_cols, col_hot, bias_block, allowed)
        scores = masked_scores(query_heads, key_heads, bias_block, allowed)
        fresh_max = jnp.maximum(run_max, jnp.max(scores, axis=-1))
        rescale = jnp.exp(run_max - fresh_max)
        weights = jnp.where(allowed[None], jnp.exp(scores - fresh_max[:, :, None]), 0.0)
        run_sum = run_sum * rescale + jnp.sum(weights, axis=-1)
        run_acc = run_acc * rescale.T[:, :, None] + jnp.einsum(
            "htu,uhd->thd",
            weights.astype(jnp.bfloat16),
            value_heads,
            preferred_element_type=jnp.float32,
        )
        run_max = fresh_max
    out_heads = (run_acc / run_sum.T[:, :, None]).astype(jnp.bfloat16)
    lse = run_max + jnp.log(run_sum)
    row_delta = jnp.sum(out_heads.astype(jnp.float32) * grad_heads.astype(jnp.float32), axis=-1).T
    out_rows = out_heads.reshape(row_count, H * DH)
    query_acc = jnp.zeros((row_count, H, DH), jnp.float32)
    key_acc = jnp.zeros((row_count, H, DH), jnp.float32)
    value_acc = jnp.zeros((row_count, H, DH), jnp.float32)
    table_acc = jnp.zeros((H, NB, NB), jnp.float32)
    for section_num in section_list:
        key_heads, value_heads, seg_cols, col_hot, bias_block, allowed = stored[section_num]
        scores = masked_scores(query_heads, key_heads, bias_block, allowed)
        probs_low, dscore = grad_terms(scores, allowed, lse, row_delta, grad_heads, value_heads)
        dscore_low = dscore.astype(jnp.bfloat16)
        query_acc = (
            query_acc
            + jnp.einsum("htu,uhd->thd", dscore_low, key_heads, preferred_element_type=jnp.float32)
            * 0.125
        )
        block_sums = dscore.reshape(H, block_count, BLK, block_count, BLK).sum(axis=(2, 4))
        table_acc = table_acc + jnp.einsum(
            "bn,hbc,cm->hnm",
            own_hot_wide,
            block_sums,
            col_hot.astype(jnp.float32),
            precision=lax.Precision.HIGHEST,
        )
        if section_num == 0:
            key_acc = (
                jnp.einsum(
                    "htu,thd->uhd", dscore_low, query_heads, preferred_element_type=jnp.float32
                )
                * 0.125
            )
            value_acc = jnp.einsum(
                "htu,thd->uhd", probs_low, grad_heads, preferred_element_type=jnp.float32
            )
        else:
            key_term = (
                jnp.einsum(
                    "htu,thd->uhd", dscore_low, query_heads, preferred_element_type=jnp.float32
                )
                * 0.125
            ).astype(jnp.bfloat16)
            value_term = jnp.einsum(
                "htu,thd->uhd", probs_low, grad_heads, preferred_element_type=jnp.float32
            ).astype(jnp.bfloat16)
            back_keys, back_values = from_partner(
                (key_term.reshape(row_count, H * DH), value_term.reshape(row_count, H * DH)),
                "seq",
                section_num - 1,
            )
            key_acc = key_acc + back_keys.reshape(row_count, H, DH).astype(jnp.float32)
            value_acc = value_acc + back_values.reshape(row_count, H, DH).astype(jnp.float32)
    table_total = lax.psum(table_acc, ("seq", "dp"))
    feature_count = H * DH
    return (
        out_rows.reshape(1, row_count, feature_count),
        query_acc.astype(jnp.bfloat16).reshape(1, row_count, feature_count),
        key_acc.astype(jnp.bfloat16).reshape(1, row_count, feature_count),
        value_acc.astype(jnp.bfloat16).reshape(1, row_count, feature_count),
        table_total,
    )


def solution(mesh):
    in_specs = (
        P("dp", "seq", None),
        P("dp", "seq", None),
        P("dp", "seq", None),
        P("dp", "seq", None),
        P("dp", "seq"),
        P("dp", "seq"),
        P("dp", "seq", None, None),
        P(),
    )
    out_specs = (
        P("dp", "seq", None),
        P("dp", "seq", None),
        P("dp", "seq", None),
        P("dp", "seq", None),
        P(),
    )
    return jax.shard_map(local, mesh=mesh, in_specs=in_specs, out_specs=out_specs, check_vma=False)
```

profile of v0, /device:TPU:0, one launch (start us, length us, event | category | flops | bytes accessed | tf_op | source)
XLA Modules:
  0.0 256.8 jit_solution(7733567742736410515)
XLA Ops:
  8.0 3.0 %collective-permute-start.4 = (bf16[128]{0:T(256)(128)(2,1)S(1)}, bf16[128]{0:T(256)(128)(2,1)S(1)}, u32[]{:S(2)}, u32[]{:S(2)}) collective-permute-start(bf16[128]{0:T(256)(128)(2,1)S(1)} %get-tuple-element.40), channel_id=1, source_target_pairs={{0,4},{2,6},{4,0},{6,2},{8,12},{10,14},{12,8},{14,10},{16,20},{18,... | collective-permute-start | bytes 776 | tf_op jit(solution)/shard_map/ppermute | solution.py:16
  10.9 1.6 collective-permute-start.8
  12.5 2.6 %collective-permute-start.12 = (bf16[128]{0:T(256)(128)(2,1)S(1)}, bf16[128]{0:T(256)(128)(2,1)S(1)}, u32[]{:S(2)}, u32[]{:S(2)}) collective-permute-start(bf16[128]{0:T(256)(128)(2,1)S(1)} %get-tuple-element.40), channel_id=1, source_target_pairs={{0,16},{2,18},{4,20},{6,22},{8,24},{10,26},{12,28},{14,30},{16,0},... | collective-permute-start | bytes 776 | tf_op jit(solution)/shard_map/ppermute | solution.py:16
  15.8 1.7 collective-permute-start.14
  22.0 1.1 copy.67
  23.2 1.8 collective-permute-start.10
  26.7 1.8 collective-permute-start.6
  31.8 2.6 %collective-permute-start.13 = (bf16[128,1024]{1,0:T(8,128)(2,1)}, bf16[128,1024]{1,0:T(8,128)(2,1)S(1)}, u32[]{:S(2)}, u32[]{:S(2)}) collective-permute-start(bf16[128,1024]{1,0:T(8,128)(2,1)} %bitcast.15), channel_id=1, source_target_pairs={{0,16},{2,18},{4,20},{6,22},{8,24},{10,26},{12,28},{14,30},{16,0},... | collective-permute-start | bytes 786440 | tf_op jit(solution)/shard_map/ppermute | solution.py:16
  36.4 1.2 collective-permute-start.5
  38.0 2.6 %broadcast_compare_fusion = (pred[128,128]{0,1:T(8,128)(4,1)S(1)}, pred[128,128]{0,1:T(8,128)(4,1)S(1)}, pred[128,128]{0,1:T(8,128)(4,1)S(1)}, pred[128,128]{0,1:T(8,128)(4,1)S(1)}, pred[128,128]{0,1:T(8,128)(4,1)S(1)}) fusion(f32[128]{0:T(128)S(1)} %get-tuple-element.41, pred[]{:T(512)} %bitcast.25, f32[128]{0:T(128)S(1)} %convert_element_type.245, ...), kind=kLoop, calls=%fused_computation.151 | loop fusion | flops 147456 | bytes 84484 | tf_op jit(solution)/shard_map/eq | solution.py:43
  41.1 6.8 %collective-permute-done.13 = bf16[128,1024]{1,0:T(8,128)(2,1)S(1)} collective-permute-done((bf16[128,1024]{1,0:T(8,128)(2,1)}, bf16[128,1024]{1,0:T(8,128)(2,1)S(1)}, u32[]{:S(2)}, u32[]{:S(2)}) %collective-permute-start.13) | collective-permute-done | bytes 262176 | tf_op jit(solution)/shard_map/ppermute | solution.py:16
  48.7 1.3 fusion.150
  50.2 1.2 collective-permute-start.7
  51.4 1.8 copy.75
  53.2 2.3 fusion.151
  55.5 1.8 copy.72
  57.3 2.3 fusion.152
  59.6 1.8 copy.69
  61.4 1.5 fusion.153
  66.0 1.8 copy.79
  67.8 2.0 convolution_bitcast_fusion
  69.9 1.8 copy.76
  71.7 2.4 convolution_bitcast_fusion.1
  74.1 1.8 copy.73
  75.8 2.4 convolution_bitcast_fusion.2
  78.3 1.8 copy.70
  80.8 3.1 %multiply_reduce_fusion = (f32[128,16]{0,1:T(8,128)S(1)}, bf16[128,16,64]{0,2,1:T(8,128)(2,1)}) fusion(bf16[128,16,64]{0,2,1:T(8,128)(2,1)S(1)} %bitcast.299, f32[128,16]{0,1:T(8,128)S(1)} %copy-done.24, f32[128,16,64]{0,2,1:T(8,128)} %convolution_bitcast_fusion, f32[128,16]{0,1:T(8,128)S(1)} %copy-done.27, f32[128,16,64]{0,2,1:T(8,128)} %convolution_bitcast_fusion.1, ...), kind=kOutput, calls=%fused_computation.103 | convolution fusion | flops 36042752 | bytes 3997696 | tf_op jit(solution)/shard_map/htu,uhd->thd/dot_general | solution.py:112
  87.0 1.3 fusion.156
  88.3 1.3 fusion.157
  90.7 1.2 fusion.32
  92.9 1.2 fusion.31
  95.6 1.2 convolution_convert_fusion
  96.8 1.2 convolution_convert_fusion.1
  98.0 1.2 convolution_convert_fusion.2
  99.8 1.9 copy.102
  101.6 1.2 fusion.29
  103.9 1.2 fusion.30
  106.1 1.9 copy.103
  108.0 2.9 %collective-permute-start.19 = (bf16[128,1024]{0,1:T(8,128)(2,1)}, bf16[128,1024]{0,1:T(8,128)(2,1)}, u32[]{:S(2)}, u32[]{:S(2)}) collective-permute-start(bf16[128,1024]{0,1:T(8,128)(2,1)} %bitcast.353), channel_id=1, source_target_pairs={{0,16},{2,18},{4,20},{6,22},{8,24},{10,26},{12,28},{14,30},{16,0},... | collective-permute-start | bytes 786440 | tf_op jit(solution)/shard_map/ppermute | solution.py:16
  111.7 2.0 collective-permute-start.23
  113.8 1.5 multiply_add_fusion
  115.9 8.2 %collective-permute-done.19 = bf16[128,1024]{0,1:T(8,128)(2,1)} collective-permute-done((bf16[128,1024]{0,1:T(8,128)(2,1)}, bf16[128,1024]{0,1:T(8,128)(2,1)}, u32[]{:S(2)}, u32[]{:S(2)}) %collective-permute-start.19) | collective-permute-done | bytes 262176 | tf_op jit(solution)/shard_map/ppermute | solution.py:16
  124.6 1.2 collective-permute-start.21
  125.8 1.4 fusion.61
  127.2 9.0 %collective-permute-done.23 = bf16[128,1024]{0,1:T(8,128)(2,1)S(1)} collective-permute-done((bf16[128,1024]{0,1:T(8,128)(2,1)}, bf16[128,1024]{0,1:T(8,128)(2,1)S(1)}, u32[]{:S(2)}, u32[]{:S(2)}) %collective-permute-start.23) | collective-permute-done | bytes 262176 | tf_op jit(solution)/shard_map/ppermute | solution.py:16
  136.2 1.1 collective-permute-done.22
  139.2 108.9 %all-reduce.2.cloned.1.call-done = f32[16,64,64]{2,1,0:T(8,128)} async-done(((f32[16,64,64]{2,1,0:T(8,128)}), f32[16,64,64]{2,1,0:T(8,128)}) %all-reduce.2.cloned.1.call-update) | async-done | bytes 262160 | tf_op jit(solution)/shard_map/psum | solution.py:172
  248.1 1.9 copy.134
  (146 shorter events, 28.7 us)
Async XLA Ops:
  7.2 12.0 %copy-start = (bf16[16,64,64]{2,1,0:T(8,128)(2,1)S(1)}, bf16[16,64,64]{2,1,0:T(8,128)(2,1)}, u32[]{:S(2)}) copy-start(bf16[16,64,64]{2,1,0:T(8,128)(2,1)} %param.15) | copy-start | bytes 393220
  7.2 240.9 %all-reduce.2.cloned.1.call-start = ((), (), s32[]{:S(2)}) async-start(), calls=%async_computation | async-start | bytes 1048576 | tf_op jit(solution)/shard_map/psum | solution.py:172
  8.0 27.9 %collective-permute-start.4 = (bf16[128]{0:T(256)(128)(2,1)S(1)}, bf16[128]{0:T(256)(128)(2,1)S(1)}, u32[]{:S(2)}, u32[]{:S(2)}) collective-permute-start(bf16[128]{0:T(256)(128)(2,1)S(1)} %get-tuple-element.40), channel_id=1, source_target_pairs={{0,4},{2,6},{4,0},{6,2},{8,12},{10,14},{12,8},{14,10},{16,20},{18,... | collective-permute-start | bytes 776 | tf_op jit(solution)/shard_map/ppermute | solution.py:16
  10.9 25.5 %collective-permute-start.8 = (bf16[128]{0:T(256)(128)(2,1)S(1)}, bf16[128]{0:T(256)(128)(2,1)S(1)}, u32[]{:S(2)}, u32[]{:S(2)}) collective-permute-start(bf16[128]{0:T(256)(128)(2,1)S(1)} %get-tuple-element.40), channel_id=1, source_target_pairs={{0,8},{2,10},{4,12},{6,14},{8,0},{10,2},{12,4},{14,6},{16,24},{18,... | collective-permute-start | bytes 776 | tf_op jit(solution)/shard_map/ppermute | solution.py:16
  12.5 25.1 %collective-permute-start.12 = (bf16[128]{0:T(256)(128)(2,1)S(1)}, bf16[128]{0:T(256)(128)(2,1)S(1)}, u32[]{:S(2)}, u32[]{:S(2)}) collective-permute-start(bf16[128]{0:T(256)(128)(2,1)S(1)} %get-tuple-element.40), channel_id=1, source_target_pairs={{0,16},{2,18},{4,20},{6,22},{8,24},{10,26},{12,28},{14,30},{16,0},... | collective-permute-start | bytes 776 | tf_op jit(solution)/shard_map/ppermute | solution.py:16
  15.1 22.5 %collective-permute-start = (bf16[128]{0:T(256)(128)(2,1)S(1)}, bf16[128]{0:T(256)(128)(2,1)S(1)}, u32[]{:S(2)}, u32[]{:S(2)}) collective-permute-start(bf16[128]{0:T(256)(128)(2,1)S(1)} %get-tuple-element.40), channel_id=1, source_target_pairs={{0,2},{2,0},{4,6},{6,4},{8,10},{10,8},{12,14},{14,12},{16,18},{18,... | collective-permute-start | bytes 776 | tf_op jit(solution)/shard_map/ppermute | solution.py:16
  15.8 7.4 %collective-permute-start.14 = (bf16[1]{0:T(256)(128)(2,1)}, bf16[1]{0:T(256)(128)(2,1)}, u32[]{:S(2)}, u32[]{:S(2)}) collective-permute-start(bf16[1]{0:T(256)(128)(2,1)} %bitcast.17), channel_id=1, source_target_pairs={{0,16},{2,18},{4,20},{6,22},{8,24},{10,26},{12,28},{14,30},{16,0},... | collective-permute-start | bytes 14 | tf_op jit(solution)/shard_map/ppermute | solution.py:16
  23.2 3.6 %collective-permute-start.10 = (bf16[1]{0:T(256)(128)(2,1)}, bf16[1]{0:T(256)(128)(2,1)}, u32[]{:S(2)}, u32[]{:S(2)}) collective-permute-start(bf16[1]{0:T(256)(128)(2,1)} %bitcast.17), channel_id=1, source_target_pairs={{0,8},{2,10},{4,12},{6,14},{8,0},{10,2},{12,4},{14,6},{16,24},{18,... | collective-permute-start | bytes 14 | tf_op jit(solution)/shard_map/ppermute | solution.py:16
  26.7 3.5 %collective-permute-start.6 = (bf16[1]{0:T(256)(128)(2,1)}, bf16[1]{0:T(256)(128)(2,1)}, u32[]{:S(2)}, u32[]{:S(2)}) collective-permute-start(bf16[1]{0:T(256)(128)(2,1)} %bitcast.17), channel_id=1, source_target_pairs={{0,4},{2,6},{4,0},{6,2},{8,12},{10,14},{12,8},{14,10},{16,20},{18,... | collective-permute-start | bytes 14 | tf_op jit(solution)/shard_map/ppermute | solution.py:16
  30.2 1.6 collective-permute-start.2
  31.8 16.0 %collective-permute-start.13 = (bf16[128,1024]{1,0:T(8,128)(2,1)}, bf16[128,1024]{1,0:T(8,128)(2,1)S(1)}, u32[]{:S(2)}, u32[]{:S(2)}) collective-permute-start(bf16[128,1024]{1,0:T(8,128)(2,1)} %bitcast.15), channel_id=1, source_target_pairs={{0,16},{2,18},{4,20},{6,22},{8,24},{10,26},{12,28},{14,30},{16,0},... | collective-permute-start | bytes 786440 | tf_op jit(solution)/shard_map/ppermute | solution.py:16
  35.8 14.4 %collective-permute-start.9 = (bf16[128,1024]{1,0:T(8,128)(2,1)}, bf16[128,1024]{1,0:T(8,128)(2,1)}, u32[]{:S(2)}, u32[]{:S(2)}) collective-permute-start(bf16[128,1024]{1,0:T(8,128)(2,1)} %bitcast.15), channel_id=1, source_target_pairs={{0,8},{2,10},{4,12},{6,14},{8,0},{10,2},{12,4},{14,6},{16,24},{18,... | collective-permute-start | bytes 786440 | tf_op jit(solution)/shard_map/ppermute | solution.py:16
  36.4 19.1 %collective-permute-start.5 = (bf16[128,1024]{1,0:T(8,128)(2,1)}, bf16[128,1024]{1,0:T(8,128)(2,1)}, u32[]{:S(2)}, u32[]{:S(2)}) collective-permute-start(bf16[128,1024]{1,0:T(8,128)(2,1)} %bitcast.15), channel_id=1, source_target_pairs={{0,4},{2,6},{4,0},{6,2},{8,12},{10,14},{12,8},{14,10},{16,20},{18,... | collective-permute-start | bytes 786440 | tf_op jit(solution)/shard_map/ppermute | solution.py:16
  37.6 22.0 %collective-permute-start.1 = (bf16[128,1024]{1,0:T(8,128)(2,1)}, bf16[128,1024]{1,0:T(8,128)(2,1)}, u32[]{:S(2)}, u32[]{:S(2)}) collective-permute-start(bf16[128,1024]{1,0:T(8,128)(2,1)} %bitcast.15), channel_id=1, source_target_pairs={{0,2},{2,0},{4,6},{6,4},{8,10},{10,8},{12,14},{14,12},{16,18},{18,... | collective-permute-start | bytes 786440 | tf_op jit(solution)/shard_map/ppermute | solution.py:16
  37.6 28.4 %collective-permute-start.15 = (bf16[128,1024]{1,0:T(8,128)(2,1)}, bf16[128,1024]{1,0:T(8,128)(2,1)}, u32[]{:S(2)}, u32[]{:S(2)}) collective-permute-start(bf16[128,1024]{1,0:T(8,128)(2,1)} %bitcast.22), channel_id=1, source_target_pairs={{0,16},{2,18},{4,20},{6,22},{8,24},{10,26},{12,28},{14,30},{16,0},... | collective-permute-start | bytes 786440 | tf_op jit(solution)/shard_map/ppermute | solution.py:16
  47.8 22.0 %collective-permute-start.11 = (bf16[128,1024]{1,0:T(8,128)(2,1)}, bf16[128,1024]{1,0:T(8,128)(2,1)}, u32[]{:S(2)}, u32[]{:S(2)}) collective-permute-start(bf16[128,1024]{1,0:T(8,128)(2,1)} %bitcast.22), channel_id=1, source_target_pairs={{0,8},{2,10},{4,12},{6,14},{8,0},{10,2},{12,4},{14,6},{16,24},{18,... | collective-permute-start | bytes 786440 | tf_op jit(solution)/shard_map/ppermute | solution.py:16
  50.2 23.9 %collective-permute-start.7 = (bf16[128,1024]{1,0:T(8,128)(2,1)}, bf16[128,1024]{1,0:T(8,128)(2,1)}, u32[]{:S(2)}, u32[]{:S(2)}) collective-permute-start(bf16[128,1024]{1,0:T(8,128)(2,1)} %bitcast.22), channel_id=1, source_target_pairs={{0,4},{2,6},{4,0},{6,2},{8,12},{10,14},{12,8},{14,10},{16,20},{18,... | collective-permute-start | bytes 786440 | tf_op jit(solution)/shard_map/ppermute | solution.py:16
  55.5 22.8 %collective-permute-start.3 = (bf16[128,1024]{1,0:T(8,128)(2,1)}, bf16[128,1024]{1,0:T(8,128)(2,1)}, u32[]{:S(2)}, u32[]{:S(2)}) collective-permute-start(bf16[128,1024]{1,0:T(8,128)(2,1)} %bitcast.22), channel_id=1, source_target_pairs={{0,2},{2,0},{4,6},{6,4},{8,10},{10,8},{12,14},{14,12},{16,18},{18,... | collective-permute-start | bytes 786440 | tf_op jit(solution)/shard_map/ppermute | solution.py:16
  61.4 1.7 copy-start.1
  61.4 1.7 copy-start.3
  78.3 1.8 copy-start.25
  78.3 1.8 copy-start.26
  78.3 1.8 copy-start.27
  80.8 3.1 %copy-start.18 = (bf16[128,1024]{0,1:T(8,128)(2,1)S(1)}, bf16[128,1024]{0,1:T(8,128)(2,1)}, u32[]{:S(2)}) copy-start(bf16[128,1024]{0,1:T(8,128)(2,1)} %copy.79) | copy-start | bytes 786436
  83.9 1.3 copy-start.19
  85.7 1.2 copy-start.6
  85.7 1.3 copy-start.23
  87.0 1.3 copy-start.4
  87.0 1.3 copy-start.17
  88.3 1.3 copy-start.14
  99.8 1.9 copy-start.9
  102.8 2.2 copy-start.13
  105.1 8.6 %copy-start.28 = (f32[64]{0:T(128)S(1)}, f32[64]{0:T(128)}, u32[]{:S(2)}) copy-start(f32[64]{0:T(128)} %fusion.128) | copy-start | bytes 772
  105.1 8.7 %copy-start.29 = (f32[64]{0:T(128)S(1)}, f32[64]{0:T(128)}, u32[]{:S(2)}) copy-start(f32[64]{0:T(128)} %get-tuple-element.68) | copy-start | bytes 772
  105.1 8.7 %copy-start.30 = (f32[64]{0:T(128)S(1)}, f32[64]{0:T(128)}, u32[]{:S(2)}) copy-start(f32[64]{0:T(128)} %get-tuple-element.69) | copy-start | bytes 772
  105.1 8.7 %copy-start.31 = (f32[64]{0:T(128)S(1)}, f32[64]{0:T(128)}, u32[]{:S(2)}) copy-start(f32[64]{0:T(128)} %get-tuple-element.70) | copy-start | bytes 772
  105.1 8.7 %copy-start.32 = (f32[64]{0:T(128)S(1)}, f32[64]{0:T(128)}, u32[]{:S(2)}) copy-start(f32[64]{0:T(128)} %get-tuple-element.71) | copy-start | bytes 772
  106.1 9.3 %copy-start.7 = (f32[16,128,128]{1,2,0:T(8,128)S(1)}, f32[16,128,128]{1,2,0:T(8,128)}, u32[]{:S(2)}) copy-start(f32[16,128,128]{1,2,0:T(8,128)} %copy-done.5) | copy-start | bytes 3145732
  108.0 16.1 %collective-permute-start.19 = (bf16[128,1024]{0,1:T(8,128)(2,1)}, bf16[128,1024]{0,1:T(8,128)(2,1)}, u32[]{:S(2)}, u32[]{:S(2)}) collective-permute-start(bf16[128,1024]{0,1:T(8,128)(2,1)} %bitcast.353), channel_id=1, source_target_pairs={{0,16},{2,18},{4,20},{6,22},{8,24},{10,26},{12,28},{14,30},{16,0},... | collective-permute-start | bytes 786440 | tf_op jit(solution)/shard_map/ppermute | solution.py:16
  110.9 13.7 %collective-permute-start.18 = (bf16[128,1024]{0,1:T(8,128)(2,1)}, bf16[128,1024]{0,1:T(8,128)(2,1)}, u32[]{:S(2)}, u32[]{:S(2)}) collective-permute-start(bf16[128,1024]{0,1:T(8,128)(2,1)} %bitcast.352), channel_id=1, source_target_pairs={{0,8},{2,10},{4,12},{6,14},{8,0},{10,2},{12,4},{14,6},{16,24},{18,... | collective-permute-start | bytes 786440 | tf_op jit(solution)/shard_map/ppermute | solution.py:16
  110.9 15.0 %collective-permute-start.17 = (bf16[128,1024]{0,1:T(8,128)(2,1)}, bf16[128,1024]{0,1:T(8,128)(2,1)}, u32[]{:S(2)}, u32[]{:S(2)}) collective-permute-start(bf16[128,1024]{0,1:T(8,128)(2,1)} %bitcast.355), channel_id=1, source_target_pairs={{0,4},{2,6},{4,0},{6,2},{8,12},{10,14},{12,8},{14,10},{16,20},{18,... | collective-permute-start | bytes 786440 | tf_op jit(solution)/shard_map/ppermute | solution.py:16
  111.7 14.1 %collective-permute-start.16 = (bf16[128,1024]{0,1:T(8,128)(2,1)}, bf16[128,1024]{0,1:T(8,128)(2,1)}, u32[]{:S(2)}, u32[]{:S(2)}) collective-permute-start(bf16[128,1024]{0,1:T(8,128)(2,1)} %bitcast.354), channel_id=1, source_target_pairs={{0,2},{2,0},{4,6},{6,4},{8,10},{10,8},{12,14},{14,12},{16,18},{18,... | collective-permute-start | bytes 786440 | tf_op jit(solution)/shard_map/ppermute | solution.py:16
  111.7 24.5 %collective-permute-start.23 = (bf16[128,1024]{0,1:T(8,128)(2,1)}, bf16[128,1024]{0,1:T(8,128)(2,1)S(1)}, u32[]{:S(2)}, u32[]{:S(2)}) collective-permute-start(bf16[128,1024]{0,1:T(8,128)(2,1)} %bitcast.343), channel_id=1, source_target_pairs={{0,16},{2,18},{4,20},{6,22},{8,24},{10,26},{12,28},{14,30},{16,0},... | collective-permute-start | bytes 786440 | tf_op jit(solution)/shard_map/ppermute | solution.py:16
  115.4 8.7 %copy-start.21 = (bf16[16,128,64]{1,2,0:T(8,128)(2,1)S(1)}, bf16[16,128,64]{1,2,0:T(8,128)(2,1)}, u32[]{:S(2)}) copy-start(bf16[16,128,64]{1,2,0:T(8,128)(2,1)} %convolution_convert_fusion.1) | copy-start | bytes 786436
  115.4 9.2 %copy-start.20 = (bf16[16,128,64]{1,2,0:T(8,128)(2,1)S(1)}, bf16[16,128,64]{1,2,0:T(8,128)(2,1)}, u32[]{:S(2)}) copy-start(bf16[16,128,64]{1,2,0:T(8,128)(2,1)} %convolution_convert_fusion.2) | copy-start | bytes 786436
  124.1 13.2 %collective-permute-start.22 = (bf16[128,1024]{0,1:T(8,128)(2,1)S(1)}, bf16[128,1024]{0,1:T(8,128)(2,1)S(1)}, u32[]{:S(2)}, u32[]{:S(2)}) collective-permute-start(bf16[128,1024]{0,1:T(8,128)(2,1)S(1)} %bitcast.342), channel_id=1, source_target_pairs={{0,8},{2,10},{4,12},{6,14},{8,0},{10,2},{12,4},{14,6},{16,24},{18,... | collective-permute-start | bytes 786440 | tf_op jit(solution)/shard_map/ppermute | solution.py:16
  124.6 12.7 %collective-permute-start.21 = (bf16[128,1024]{0,1:T(8,128)(2,1)S(1)}, bf16[128,1024]{0,1:T(8,128)(2,1)S(1)}, u32[]{:S(2)}, u32[]{:S(2)}) collective-permute-start(bf16[128,1024]{0,1:T(8,128)(2,1)S(1)} %bitcast.341), channel_id=1, source_target_pairs={{0,4},{2,6},{4,0},{6,2},{8,12},{10,14},{12,8},{14,10},{16,20},{18,... | collective-permute-start | bytes 786440 | tf_op jit(solution)/shard_map/ppermute | solution.py:16
  125.8 11.5 %collective-permute-start.20 = (bf16[128,1024]{0,1:T(8,128)(2,1)S(1)}, bf16[128,1024]{0,1:T(8,128)(2,1)S(1)}, u32[]{:S(2)}, u32[]{:S(2)}) collective-permute-start(bf16[128,1024]{0,1:T(8,128)(2,1)S(1)} %bitcast.345), channel_id=1, source_target_pairs={{0,2},{2,0},{4,6},{6,4},{8,10},{10,8},{12,14},{14,12},{16,18},{18,... | collective-permute-start | bytes 786440 | tf_op jit(solution)/shard_map/ppermute | solution.py:16
  (11 other events, 11.5 us)
Sparse Core Ops, SparseCore 0:
  115.5 132.5 all-reduce.1
where the time goes:
time: 258 us; the launch traced here: 257 us
  waiting for transfers between devices  136 us (53%)
  matrix products  38.1 us (15%)
  local copies, waits for them, and re-layouts  28.9 us (11%)
  starting transfers between devices  26.2 us (10%)
  between operations  17.7 us (7%)
  other arithmetic  9.98 us (4%)
    psum x1, waiting for transfers between devices, local(): table_total = lax.psum(table_acc, ('seq', 'dp'))  109 us
    ppermute x24, waiting for transfers between devices, from_partner(): return lax.ppermute(value, axis, pairs)  27.1 us
    ppermute x24, starting transfers between devices, from_partner(): return lax.ppermute(value, axis, pairs)  26.2 us
    unnamed x77, local copies, waits for them, and re-layouts  14.8 us
    ppermute x8, local copies, waits for them, and re-layouts, from_partner(): return lax.ppermute(value, axis, pairs)  13.4 us
    dot_general x5, matrix products, local(): jnp.einsum('htu,uhd->thd', weights.astype(jnp.bfloat16), value_heads, pre...  11 us
    dot_general x5, matrix products, masked_scores(): jnp.einsum('thd,uhd->htu', query_heads, key_heads, preferred_element_type...  7.82 us
  transfers between devices with their start and end apart: 25, of which 9 were waited for; matrix products, arithmetic and copies ran while one was open for 17% of the time, Pallas kernels for 0%

commit v1 on v0

--- a/solution.py
+++ b/solution.py
@@ -169,7 +169,7 @@
             )
             key_acc = key_acc + back_keys.reshape(row_count, H, DH).astype(jnp.float32)
             value_acc = value_acc + back_values.reshape(row_count, H, DH).astype(jnp.float32)
-    table_total = lax.psum(table_acc, ("seq", "dp"))
+    table_total = jnp.sum(lax.all_gather(table_acc, ("seq", "dp")), axis=0)
     feature_count = H * DH
     return (
         out_rows.reshape(1, row_count, feature_count),

time: 258 us -> 241 us (0.934)
  waiting for transfers between devices: 136 us -> 97 us
  other arithmetic: 9.98 us -> 24.1 us
  matrix products: 38.1 us -> 51.5 us
  local copies, waits for them, and re-layouts: 28.9 us -> 21.6 us
    psum x1 -> x0, waiting for transfers between devices: 109 us -> none  [local(): table_total = lax.psum(table_acc, ('seq', 'dp'))]
    all_gather x0 -> x1, waiting for transfers between devices: none -> 81.5 us  [local(): table_total = jnp.sum(lax.all_gather(table_acc, ('seq', 'dp')), axis=0)]
    ppermute x24, waiting for transfers between devices: 27.1 us -> 15.5 us  [from_partner(): return lax.ppermute(value, axis, pairs)]
    reduce_sum x0 -> x1, other arithmetic: none -> 8.66 us  [local(): table_total = jnp.sum(lax.all_gather(table_acc, ('seq', 'dp')), axis=0)]
    dot_general x5, matrix products: 4.34 us -> 11.6 us  [grad_terms(): jnp.einsum('thd,uhd->htu', grad_heads, value_heads, preferred_element_typ...]
    unnamed x77 -> x26, local copies, waits for them, and re-layouts: 14.8 us -> 9.96 us
    dot_general x5, matrix products: 4.63 us -> 9.02 us  [local(): jnp.einsum('htu,thd->uhd', probs_low, grad_heads, preferred_element_type=...]
  transfers between devices with their start and end apart: 25 -> 25, of which waited for: 9 -> 7; matrix products, arithmetic and copies ran while one was open for 17% -> 28% of each run, Pallas kernels for 0% -> 0%
where the time goes in v1:
time: 241 us; the launch traced here: 240 us
  waiting for transfers between devices  97 us (40%)
  matrix products  51.5 us (21%)
  starting transfers between devices  27.9 us (12%)
  other arithmetic  24.1 us (10%)
  local copies, waits for them, and re-layouts  21.6 us (9%)
  between operations  17.6 us (7%)
    all_gather x1, waiting for transfers between devices, local(): table_total = jnp.sum(lax.all_gather(table_acc, ('seq', 'dp')), axis=0)  81.5 us
    ppermute x24, starting transfers between devices, from_partner(): return lax.ppermute(value, axis, pairs)  27.8 us
    ppermute x24, waiting for transfers between devices, from_partner(): return lax.ppermute(value, axis, pairs)  15.5 us
    dot_general x5, matrix products, grad_terms(): jnp.einsum('thd,uhd->htu', grad_heads, value_heads, preferred_element_typ...  11.6 us
    ppermute x8, local copies, waits for them, and re-layouts, from_partner(): return lax.ppermute(value, axis, pairs)  11.1 us
    dot_general x5, matrix products, local(): jnp.einsum('htu,uhd->thd', weights.astype(jnp.bfloat16), value_heads, pre...  10.9 us
    unnamed x26, local copies, waits for them, and re-layouts  9.96 us
    dot_general x5, matrix products, local(): jnp.einsum('htu,thd->uhd', probs_low, grad_heads, preferred_element_type=...  9.02 us
  transfers between devices with their start and end apart: 25, of which 7 were waited for; matrix products, arithmetic and copies ran while one was open for 28% of the time, Pallas kernels for 0%

profile of v1, /device:TPU:0, one launch (start us, length us, event | category | flops | bytes accessed | tf_op | source)
XLA Modules:
  0.0 239.8 jit_solution(3496753649328290169)
XLA Ops:
  8.0 4.0 %collective-permute-start.12 = (bf16[128]{0:T(256)(128)(2,1)S(1)}, bf16[128]{0:T(256)(128)(2,1)S(1)}, u32[]{:S(2)}, u32[]{:S(2)}) collective-permute-start(bf16[128]{0:T(256)(128)(2,1)S(1)} %get-tuple-element.45), channel_id=1, source_target_pairs={{0,16},{2,18},{4,20},{6,22},{8,24},{10,26},{12,28},{14,30},{16,0},... | collective-permute-start | bytes 776 | tf_op jit(solution)/shard_map/ppermute | solution.py:16
  12.0 1.6 collective-permute-start.8
  13.6 1.5 collective-permute-start.4
  15.8 1.7 collective-permute-start.14
  24.2 1.8 collective-permute-start.10
  27.8 1.8 collective-permute-start.6
  32.9 2.6 %collective-permute-start.13 = (bf16[128,1024]{1,0:T(8,128)(2,1)}, bf16[128,1024]{1,0:T(8,128)(2,1)}, u32[]{:S(2)}, u32[]{:S(2)}) collective-permute-start(bf16[128,1024]{1,0:T(8,128)(2,1)} %bitcast.347), channel_id=1, source_target_pairs={{0,16},{2,18},{4,20},{6,22},{8,24},{10,26},{12,28},{14,30},{16,0},... | collective-permute-start | bytes 786440 | tf_op jit(solution)/shard_map/ppermute | solution.py:16
  39.1 2.7 %broadcast_compare_fusion = (pred[128,128]{0,1:T(8,128)(4,1)S(1)}, pred[128,128]{0,1:T(8,128)(4,1)S(1)}, pred[128,128]{0,1:T(8,128)(4,1)S(1)}, pred[128,128]{0,1:T(8,128)(4,1)S(1)}, pred[128,128]{0,1:T(8,128)(4,1)S(1)}) fusion(f32[128]{0:T(128)S(1)} %get-tuple-element.46, pred[]{:T(512)} %bitcast.25, f32[128]{0:T(128)S(1)} %convert_element_type.245, ...), kind=kLoop, calls=%fused_computation.151 | loop fusion | flops 147456 | bytes 84484 | tf_op jit(solution)/shard_map/eq | solution.py:43
  42.2 1.5 collective-permute-start.11
  43.9 1.4 fusion.153
  47.6 4.3 %collective-permute-done.9 = bf16[128,1024]{1,0:T(8,128)(2,1)} collective-permute-done((bf16[128,1024]{1,0:T(8,128)(2,1)}, bf16[128,1024]{1,0:T(8,128)(2,1)}, u32[]{:S(2)}, u32[]{:S(2)}) %collective-permute-start.9) | collective-permute-done | bytes 262176 | tf_op jit(solution)/shard_map/ppermute | solution.py:16
  51.9 1.8 copy.116
  53.7 2.4 fusion.151
  56.1 1.8 copy.119
  60.4 1.6 fusion.35
  62.0 1.6 fusion.39
  66.1 1.8 copy.114
  67.9 2.0 convolution_bitcast_fusion.2
  70.0 1.8 copy.117
  71.8 2.4 convolution_bitcast_fusion.1
  74.2 1.8 copy.120
  76.0 2.4 convolution_bitcast_fusion
  78.3 1.8 copy.111
  80.1 3.0 %multiply_reduce_fusion = (f32[128,16]{0,1:T(8,128)S(1)}, bf16[128,16,64]{0,2,1:T(8,128)(2,1)}) fusion(bf16[128,16,64]{0,2,1:T(8,128)(2,1)S(1)} %bitcast.301, f32[128,16]{0,1:T(8,128)} %get-tuple-element.20, f32[128,16,64]{0,2,1:T(8,128)} %convolution_bitcast_fusion, f32[128,16]{0,1:T(8,128)} %get-tuple-element.23, ...), kind=kOutput, calls=%fused_computation.103 | convolution fusion | flops 36042752 | bytes 3997696 | tf_op jit(solution)/shard_map/htu,uhd->thd/dot_general | solution.py:112
  83.2 2.6 %fusion.156 = (f32[16]{0:T(128)S(1)}, bf16[16,128,128]{1,2,0:T(8,128)(2,1)}) fusion(f32[16,128]{1,0:T(8,128)S(1)} %bitcast.363, bf16[128,16,64]{0,2,1:T(8,128)(2,1)S(1)} %bitcast.302, bf16[128,16,64]{0,2,1:T(8,128)(2,1)} %bitcast.357, f32[16,128,128]{1,2,0:T(8,128)} %get-tuple-element.54, f32[16,128]{1,0:T(8,128)S(1)} %log_add_fusion, ...), kind=kOutput, calls=%fused_computation.229 | convolution fusion | flops 35127280 | bytes 2129984 | tf_op jit(solution)/shard_map/thd,uhd->htu/dot_general | solution.py:57
  85.8 1.5 fusion.157
  87.3 2.6 %fusion.158 = (f32[16]{0:T(128)S(1)}, bf16[16,128,128]{1,2,0:T(8,128)(2,1)}) fusion(f32[16,128]{1,0:T(8,128)S(1)} %bitcast.365, bf16[128,16,64]{0,2,1:T(8,128)(2,1)S(1)} %bitcast.304, bf16[128,16,64]{0,2,1:T(8,128)(2,1)} %bitcast.337, f32[16,128,128]{1,2,0:T(8,128)} %get-tuple-element.50, f32[16,128]{1,0:T(8,128)S(1)} %log_add_fusion, ...), kind=kOutput, calls=%fused_computation.231 | convolution fusion | flops 35127280 | bytes 2129984 | tf_op jit(solution)/shard_map/thd,uhd->htu/dot_general | solution.py:57
  89.9 2.6 %fusion.159 = (f32[16]{0:T(128)S(1)}, bf16[16,128,128]{1,2,0:T(8,128)(2,1)}) fusion(f32[16,128]{1,0:T(8,128)S(1)} %bitcast.366, bf16[128,16,64]{0,2,1:T(8,128)(2,1)S(1)} %bitcast.305, bf16[128,16,64]{0,2,1:T(8,128)(2,1)} %bitcast.339, f32[16,128,128]{1,2,0:T(8,128)} %copy-done.1, f32[16,128]{1,0:T(8,128)S(1)} %log_add_fusion, ...), kind=kOutput, calls=%fused_computation.232 | convolution fusion | flops 35127280 | bytes 2129984 | tf_op jit(solution)/shard_map/thd,uhd->htu/dot_general | solution.py:57
  92.5 2.2 fusion.155
  95.5 2.4 %multiply_add_fusion = f32[16,64,64]{2,1,0:T(8,128)} fusion(f32[64]{0:T(128)} %get-tuple-element.73, f32[16,64]{1,0:T(8,128)S(1)} %get-tuple-element.35, f32[64]{0:T(128)} %get-tuple-element.74, f32[16,64]{1,0:T(8,128)S(1)} %get-tuple-element.34, f32[64]{0:T(128)} %get-tuple-element.75, f32[16,64]{1,0:T(8,128)S(1)} %get-tuple-element.33, ...), kind=kLoop, calls=%fused_computation.102 | loop fusion | flops 589824 | bytes 283904 | tf_op jit(solution)/shard_map/add | solution.py:138
  98.0 2.5 %convolution_convert_fusion = bf16[16,128,64]{1,2,0:T(8,128)(2,1)} fusion(bf16[128,16,64]{0,2,1:T(8,128)(2,1)S(1)} %bitcast.307, f32[16,128,128]{1,2,0:T(8,128)} %copy-done.1, f32[16,128]{1,0:T(8,128)S(1)} %log_add_fusion, pred[128,128]{0,1:T(8,128)(4,1)S(1)} %get-tuple-element.39), kind=kOutput, calls=%fused_computation.56 | convolution fusion | flops 34471936 | bytes 1597440 | tf_op jit(solution)/shard_map/htu,thd->uhd/dot_general | solution.py:162
  100.5 2.4 %convolution_convert_fusion.1 = bf16[16,128,64]{1,2,0:T(8,128)(2,1)} fusion(bf16[128,16,64]{0,2,1:T(8,128)(2,1)S(1)} %bitcast.308, f32[16,128,128]{1,2,0:T(8,128)} %get-tuple-element.50, f32[16,128]{1,0:T(8,128)S(1)} %log_add_fusion, pred[128,128]{0,1:T(8,128)(4,1)S(1)} %get-tuple-element.38), kind=kOutput, calls=%fused_computation.57 | convolution fusion | flops 34471936 | bytes 1597440 | tf_op jit(solution)/shard_map/htu,thd->uhd/dot_general | solution.py:162
  105.3 2.5 %convolution_convert_fusion.3 = bf16[16,128,64]{1,2,0:T(8,128)(2,1)} fusion(bf16[128,16,64]{0,2,1:T(8,128)(2,1)S(1)} %bitcast.310, f32[16,128,128]{1,2,0:T(8,128)} %get-tuple-element.54, f32[16,128]{1,0:T(8,128)S(1)} %log_add_fusion, pred[128,128]{0,1:T(8,128)(4,1)S(1)} %get-tuple-element.40), kind=kOutput, calls=%fused_computation.59 | convolution fusion | flops 34471936 | bytes 1597440 | tf_op jit(solution)/shard_map/htu,thd->uhd/dot_general | solution.py:162
  108.0 2.2 fusion.29
  111.4 2.2 fusion.31
  113.6 1.4 fusion.96
  115.0 1.4 fusion.103
  116.4 1.4 fusion.93
  117.8 1.4 convolution_add_fusion.1
  120.4 1.8 copy.143
  123.1 1.8 collective-permute-start.18
  124.9 1.5 fusion.28
  126.4 2.9 %collective-permute-start.19 = (bf16[128,1024]{0,1:T(8,128)(2,1)S(1)}, bf16[128,1024]{0,1:T(8,128)(2,1)S(1)}, u32[]{:S(2)}, u32[]{:S(2)}) collective-permute-start(bf16[128,1024]{0,1:T(8,128)(2,1)S(1)} %bitcast.361), channel_id=1, source_target_pairs={{0,16},{2,18},{4,20},{6,22},{8,24},{10,26},{12,28},{14,30},{16,0},... | collective-permute-start | bytes 786440 | tf_op jit(solution)/shard_map/ppermute | solution.py:16
  130.2 1.4 fusion.60
  132.4 5.8 %collective-permute-done.18 = bf16[128,1024]{0,1:T(8,128)(2,1)S(1)} collective-permute-done((bf16[128,1024]{0,1:T(8,128)(2,1)}, bf16[128,1024]{0,1:T(8,128)(2,1)S(1)}, u32[]{:S(2)}, u32[]{:S(2)}) %collective-permute-start.18) | collective-permute-done | bytes 262176 | tf_op jit(solution)/shard_map/ppermute | solution.py:16
  138.2 3.5 %collective-permute-done.19 = bf16[128,1024]{0,1:T(8,128)(2,1)S(1)} collective-permute-done((bf16[128,1024]{0,1:T(8,128)(2,1)S(1)}, bf16[128,1024]{0,1:T(8,128)(2,1)S(1)}, u32[]{:S(2)}, u32[]{:S(2)}) %collective-permute-start.19) | collective-permute-done | bytes 262176 | tf_op jit(solution)/shard_map/ppermute | solution.py:16
  142.8 81.5 %all-gather.3.cloned.1.call-done = f32[512,64,64]{2,1,0:T(8,128)} async-done(((f32[16,64,64]{2,1,0:T(8,128)}), f32[512,64,64]{2,1,0:T(8,128)}) %all-gather.3.cloned.1.call-update) | async-done | bytes 8388624 | tf_op jit(solution)/shard_map/all_gather | solution.py:172
  224.3 8.7 %reduce_sum.134 = f32[16,64,64]{2,1,0:T(8,128)} reduce(f32[32,16,64,64]{3,2,1,0:T(8,128)} %bitcast.300, f32[]{:T(128)} %constant.8.clone.1), dimensions={0}, to_apply=%region_16.17 | reduce | flops 2031616 | bytes 8650756 | tf_op jit(solution)/shard_map/reduce_sum | solution.py:172
  (96 shorter events, 30.8 us)
Async XLA Ops:
  7.2 12.1 %copy-start = (bf16[16,64,64]{2,1,0:T(8,128)(2,1)S(1)}, bf16[16,64,64]{2,1,0:T(8,128)(2,1)}, u32[]{:S(2)}) copy-start(bf16[16,64,64]{2,1,0:T(8,128)(2,1)} %param.15) | copy-start | bytes 393220
  7.2 217.1 %all-gather.3.cloned.1.call-start = ((), (), s32[]{:S(2)}) async-start(), calls=%async_computation | async-start | bytes 17301504 | tf_op jit(solution)/shard_map/all_gather | solution.py:172
  8.0 28.9 %collective-permute-start.12 = (bf16[128]{0:T(256)(128)(2,1)S(1)}, bf16[128]{0:T(256)(128)(2,1)S(1)}, u32[]{:S(2)}, u32[]{:S(2)}) collective-permute-start(bf16[128]{0:T(256)(128)(2,1)S(1)} %get-tuple-element.45), channel_id=1, source_target_pairs={{0,16},{2,18},{4,20},{6,22},{8,24},{10,26},{12,28},{14,30},{16,0},... | collective-permute-start | bytes 776 | tf_op jit(solution)/shard_map/ppermute | solution.py:16
  12.0 25.4 %collective-permute-start.8 = (bf16[128]{0:T(256)(128)(2,1)S(1)}, bf16[128]{0:T(256)(128)(2,1)S(1)}, u32[]{:S(2)}, u32[]{:S(2)}) collective-permute-start(bf16[128]{0:T(256)(128)(2,1)S(1)} %get-tuple-element.45), channel_id=1, source_target_pairs={{0,8},{2,10},{4,12},{6,14},{8,0},{10,2},{12,4},{14,6},{16,24},{18,... | collective-permute-start | bytes 776 | tf_op jit(solution)/shard_map/ppermute | solution.py:16
  13.6 25.1 %collective-permute-start.4 = (bf16[128]{0:T(256)(128)(2,1)S(1)}, bf16[128]{0:T(256)(128)(2,1)S(1)}, u32[]{:S(2)}, u32[]{:S(2)}) collective-permute-start(bf16[128]{0:T(256)(128)(2,1)S(1)} %get-tuple-element.45), channel_id=1, source_target_pairs={{0,4},{2,6},{4,0},{6,2},{8,12},{10,14},{12,8},{14,10},{16,20},{18,... | collective-permute-start | bytes 776 | tf_op jit(solution)/shard_map/ppermute | solution.py:16
  15.1 23.6 %collective-permute-start = (bf16[128]{0:T(256)(128)(2,1)S(1)}, bf16[128]{0:T(256)(128)(2,1)S(1)}, u32[]{:S(2)}, u32[]{:S(2)}) collective-permute-start(bf16[128]{0:T(256)(128)(2,1)S(1)} %get-tuple-element.45), channel_id=1, source_target_pairs={{0,2},{2,0},{4,6},{6,4},{8,10},{10,8},{12,14},{14,12},{16,18},{18,... | collective-permute-start | bytes 776 | tf_op jit(solution)/shard_map/ppermute | solution.py:16
  15.8 8.5 %collective-permute-start.14 = (bf16[1]{0:T(256)(128)(2,1)}, bf16[1]{0:T(256)(128)(2,1)}, u32[]{:S(2)}, u32[]{:S(2)}) collective-permute-start(bf16[1]{0:T(256)(128)(2,1)} %bitcast.17), channel_id=1, source_target_pairs={{0,16},{2,18},{4,20},{6,22},{8,24},{10,26},{12,28},{14,30},{16,0},... | collective-permute-start | bytes 14 | tf_op jit(solution)/shard_map/ppermute | solution.py:16
  23.0 24.3 %copy-start.3 = (bf16[1,128,1024]{1,2,0:T(8,128)(2,1)}, bf16[1,128,1024]{1,2,0:T(8,128)(2,1)S(1)}, u32[]{:S(2)}) copy-start(bf16[1,128,1024]{1,2,0:T(8,128)(2,1)S(1)} %copy.107) | copy-start | bytes 786436
  24.2 59.0 %copy-start.4 = (bf16[1,128,1024]{1,2,0:T(8,128)(2,1)}, bf16[1,128,1024]{1,2,0:T(8,128)(2,1)S(1)}, u32[]{:S(2)}) copy-start(bf16[1,128,1024]{1,2,0:T(8,128)(2,1)S(1)} %copy.108) | copy-start | bytes 786436
  24.2 3.6 %collective-permute-start.10 = (bf16[1]{0:T(256)(128)(2,1)}, bf16[1]{0:T(256)(128)(2,1)}, u32[]{:S(2)}, u32[]{:S(2)}) collective-permute-start(bf16[1]{0:T(256)(128)(2,1)} %bitcast.17), channel_id=1, source_target_pairs={{0,8},{2,10},{4,12},{6,14},{8,0},{10,2},{12,4},{14,6},{16,24},{18,... | collective-permute-start | bytes 14 | tf_op jit(solution)/shard_map/ppermute | solution.py:16
  27.8 3.5 %collective-permute-start.6 = (bf16[1]{0:T(256)(128)(2,1)}, bf16[1]{0:T(256)(128)(2,1)}, u32[]{:S(2)}, u32[]{:S(2)}) collective-permute-start(bf16[1]{0:T(256)(128)(2,1)} %bitcast.17), channel_id=1, source_target_pairs={{0,4},{2,6},{4,0},{6,2},{8,12},{10,14},{12,8},{14,10},{16,20},{18,... | collective-permute-start | bytes 14 | tf_op jit(solution)/shard_map/ppermute | solution.py:16
  31.3 1.6 collective-permute-start.2
  32.9 23.2 %collective-permute-start.13 = (bf16[128,1024]{1,0:T(8,128)(2,1)}, bf16[128,1024]{1,0:T(8,128)(2,1)}, u32[]{:S(2)}, u32[]{:S(2)}) collective-permute-start(bf16[128,1024]{1,0:T(8,128)(2,1)} %bitcast.347), channel_id=1, source_target_pairs={{0,16},{2,18},{4,20},{6,22},{8,24},{10,26},{12,28},{14,30},{16,0},... | collective-permute-start | bytes 786440 | tf_op jit(solution)/shard_map/ppermute | solution.py:16
  36.8 15.1 %collective-permute-start.9 = (bf16[128,1024]{1,0:T(8,128)(2,1)}, bf16[128,1024]{1,0:T(8,128)(2,1)}, u32[]{:S(2)}, u32[]{:S(2)}) collective-permute-start(bf16[128,1024]{1,0:T(8,128)(2,1)} %bitcast.348), channel_id=1, source_target_pairs={{0,8},{2,10},{4,12},{6,14},{8,0},{10,2},{12,4},{14,6},{16,24},{18,... | collective-permute-start | bytes 786440 | tf_op jit(solution)/shard_map/ppermute | solution.py:16
  37.4 8.4 %collective-permute-start.5 = (bf16[128,1024]{1,0:T(8,128)(2,1)}, bf16[128,1024]{1,0:T(8,128)(2,1)S(1)}, u32[]{:S(2)}, u32[]{:S(2)}) collective-permute-start(bf16[128,1024]{1,0:T(8,128)(2,1)} %bitcast.349), channel_id=1, source_target_pairs={{0,4},{2,6},{4,0},{6,2},{8,12},{10,14},{12,8},{14,10},{16,20},{18,... | collective-permute-start | bytes 786440 | tf_op jit(solution)/shard_map/ppermute | solution.py:16
  38.7 3.5 %collective-permute-start.1 = (bf16[128,1024]{1,0:T(8,128)(2,1)}, bf16[128,1024]{1,0:T(8,128)(2,1)S(1)}, u32[]{:S(2)}, u32[]{:S(2)}) collective-permute-start(bf16[128,1024]{1,0:T(8,128)(2,1)} %bitcast.350), channel_id=1, source_target_pairs={{0,2},{2,0},{4,6},{6,4},{8,10},{10,8},{12,14},{14,12},{16,18},{18,... | collective-permute-start | bytes 786440 | tf_op jit(solution)/shard_map/ppermute | solution.py:16
  38.7 35.5 %collective-permute-start.15 = (bf16[128,1024]{1,0:T(8,128)(2,1)}, bf16[128,1024]{1,0:T(8,128)(2,1)}, u32[]{:S(2)}, u32[]{:S(2)}) collective-permute-start(bf16[128,1024]{1,0:T(8,128)(2,1)} %bitcast.351), channel_id=1, source_target_pairs={{0,16},{2,18},{4,20},{6,22},{8,24},{10,26},{12,28},{14,30},{16,0},... | collective-permute-start | bytes 786440 | tf_op jit(solution)/shard_map/ppermute | solution.py:16
  42.2 27.8 %collective-permute-start.11 = (bf16[128,1024]{1,0:T(8,128)(2,1)}, bf16[128,1024]{1,0:T(8,128)(2,1)}, u32[]{:S(2)}, u32[]{:S(2)}) collective-permute-start(bf16[128,1024]{1,0:T(8,128)(2,1)} %bitcast.352), channel_id=1, source_target_pairs={{0,8},{2,10},{4,12},{6,14},{8,0},{10,2},{12,4},{14,6},{16,24},{18,... | collective-permute-start | bytes 786440 | tf_op jit(solution)/shard_map/ppermute | solution.py:16
  43.9 3.3 %copy-start.5 = (bf16[128,1024]{0,1:T(8,128)(2,1)}, bf16[128,1024]{0,1:T(8,128)(2,1)S(1)}, u32[]{:S(2)}) copy-start(bf16[128,1024]{0,1:T(8,128)(2,1)S(1)} %copy.110) | copy-start | bytes 786436
  45.8 20.3 %collective-permute-start.7 = (bf16[128,1024]{1,0:T(8,128)(2,1)}, bf16[128,1024]{1,0:T(8,128)(2,1)}, u32[]{:S(2)}, u32[]{:S(2)}) collective-permute-start(bf16[128,1024]{1,0:T(8,128)(2,1)} %bitcast.353), channel_id=1, source_target_pairs={{0,4},{2,6},{4,0},{6,2},{8,12},{10,14},{12,8},{14,10},{16,20},{18,... | collective-permute-start | bytes 786440 | tf_op jit(solution)/shard_map/ppermute | solution.py:16
  47.2 36.0 %copy-start.6 = (bf16[128,1024]{0,1:T(8,128)(2,1)}, bf16[128,1024]{0,1:T(8,128)(2,1)S(1)}, u32[]{:S(2)}) copy-start(bf16[128,1024]{0,1:T(8,128)(2,1)S(1)} %copy.113) | copy-start | bytes 786436
  51.9 26.4 %collective-permute-start.3 = (bf16[128,1024]{1,0:T(8,128)(2,1)}, bf16[128,1024]{1,0:T(8,128)(2,1)}, u32[]{:S(2)}, u32[]{:S(2)}) collective-permute-start(bf16[128,1024]{1,0:T(8,128)(2,1)} %bitcast.354), channel_id=1, source_target_pairs={{0,2},{2,0},{4,6},{6,4},{8,10},{10,8},{12,14},{14,12},{16,18},{18,... | collective-permute-start | bytes 786440 | tf_op jit(solution)/shard_map/ppermute | solution.py:16
  56.1 7.6 %copy-start.8 = (f32[16,128]{1,0:T(8,128)}, f32[16,128]{1,0:T(8,128)S(1)}, u32[]{:S(2)}) copy-start(f32[16,128]{1,0:T(8,128)S(1)} %get-tuple-element.49) | copy-start | bytes 24580
  59.2 1.0 copy-start.1
  98.0 21.7 %copy-start.7 = (bf16[128,1024]{0,1:T(8,128)(2,1)S(1)}, bf16[128,1024]{0,1:T(8,128)(2,1)}, u32[]{:S(2)}) copy-start(bf16[128,1024]{0,1:T(8,128)(2,1)} %copy-done.6) | copy-start | bytes 786436
  98.0 22.0 %copy-start.2 = (bf16[16,128,128]{1,2,0:T(8,128)(2,1)S(1)}, bf16[16,128,128]{1,2,0:T(8,128)(2,1)}, u32[]{:S(2)}) copy-start(bf16[16,128,128]{1,2,0:T(8,128)(2,1)} %get-tuple-element.68) | copy-start | bytes 1572868
  100.5 25.9 %collective-permute-start.23 = (bf16[128,1024]{0,1:T(8,128)(2,1)}, bf16[128,1024]{0,1:T(8,128)(2,1)}, u32[]{:S(2)}, u32[]{:S(2)}) collective-permute-start(bf16[128,1024]{0,1:T(8,128)(2,1)} %bitcast.84), channel_id=1, source_target_pairs={{0,16},{2,18},{4,20},{6,22},{8,24},{10,26},{12,28},{14,30},{16,0},... | collective-permute-start | bytes 786440 | tf_op jit(solution)/shard_map/ppermute | solution.py:16
  102.9 26.4 %collective-permute-start.22 = (bf16[128,1024]{0,1:T(8,128)(2,1)}, bf16[128,1024]{0,1:T(8,128)(2,1)}, u32[]{:S(2)}, u32[]{:S(2)}) collective-permute-start(bf16[128,1024]{0,1:T(8,128)(2,1)} %bitcast.81), channel_id=1, source_target_pairs={{0,8},{2,10},{4,12},{6,14},{8,0},{10,2},{12,4},{14,6},{16,24},{18,... | collective-permute-start | bytes 786440 | tf_op jit(solution)/shard_map/ppermute | solution.py:16
  104.1 26.1 %collective-permute-start.21 = (bf16[128,1024]{0,1:T(8,128)(2,1)}, bf16[128,1024]{0,1:T(8,128)(2,1)}, u32[]{:S(2)}, u32[]{:S(2)}) collective-permute-start(bf16[128,1024]{0,1:T(8,128)(2,1)} %bitcast.78), channel_id=1, source_target_pairs={{0,4},{2,6},{4,0},{6,2},{8,12},{10,14},{12,8},{14,10},{16,20},{18,... | collective-permute-start | bytes 786440 | tf_op jit(solution)/shard_map/ppermute | solution.py:16
  107.8 22.4 %collective-permute-start.20 = (bf16[128,1024]{0,1:T(8,128)(2,1)}, bf16[128,1024]{0,1:T(8,128)(2,1)}, u32[]{:S(2)}, u32[]{:S(2)}) collective-permute-start(bf16[128,1024]{0,1:T(8,128)(2,1)} %bitcast.75), channel_id=1, source_target_pairs={{0,2},{2,0},{4,6},{6,4},{8,10},{10,8},{12,14},{14,12},{16,18},{18,... | collective-permute-start | bytes 786440 | tf_op jit(solution)/shard_map/ppermute | solution.py:16
  123.1 15.1 %collective-permute-start.18 = (bf16[128,1024]{0,1:T(8,128)(2,1)}, bf16[128,1024]{0,1:T(8,128)(2,1)S(1)}, u32[]{:S(2)}, u32[]{:S(2)}) collective-permute-start(bf16[128,1024]{0,1:T(8,128)(2,1)} %bitcast.360), channel_id=1, source_target_pairs={{0,8},{2,10},{4,12},{6,14},{8,0},{10,2},{12,4},{14,6},{16,24},{18,... | collective-permute-start | bytes 786440 | tf_op jit(solution)/shard_map/ppermute | solution.py:16
  126.4 15.4 %collective-permute-start.19 = (bf16[128,1024]{0,1:T(8,128)(2,1)S(1)}, bf16[128,1024]{0,1:T(8,128)(2,1)S(1)}, u32[]{:S(2)}, u32[]{:S(2)}) collective-permute-start(bf16[128,1024]{0,1:T(8,128)(2,1)S(1)} %bitcast.361), channel_id=1, source_target_pairs={{0,16},{2,18},{4,20},{6,22},{8,24},{10,26},{12,28},{14,30},{16,0},... | collective-permute-start | bytes 786440 | tf_op jit(solution)/shard_map/ppermute | solution.py:16
  129.3 12.4 %collective-permute-start.17 = (bf16[128,1024]{0,1:T(8,128)(2,1)}, bf16[128,1024]{0,1:T(8,128)(2,1)S(1)}, u32[]{:S(2)}, u32[]{:S(2)}) collective-permute-start(bf16[128,1024]{0,1:T(8,128)(2,1)} %bitcast.359), channel_id=1, source_target_pairs={{0,4},{2,6},{4,0},{6,2},{8,12},{10,14},{12,8},{14,10},{16,20},{18,... | collective-permute-start | bytes 786440 | tf_op jit(solution)/shard_map/ppermute | solution.py:16
  130.2 11.6 %collective-permute-start.16 = (bf16[128,1024]{0,1:T(8,128)(2,1)}, bf16[128,1024]{0,1:T(8,128)(2,1)S(1)}, u32[]{:S(2)}, u32[]{:S(2)}) collective-permute-start(bf16[128,1024]{0,1:T(8,128)(2,1)} %bitcast.358), channel_id=1, source_target_pairs={{0,2},{2,0},{4,6},{6,4},{8,10},{10,8},{12,14},{14,12},{16,18},{18,... | collective-permute-start | bytes 786440 | tf_op jit(solution)/shard_map/ppermute | solution.py:16
Sparse Core Ops, SparseCore 0:
  98.1 126.1 all-gather.2
